TPU v7x, 256 devices: a whole 4x4x8 slice. The times are simulated.
256 devices in a mesh: cube: 4 (over y), row: 4 (over x), col: 16 (over z, core).
Axes of the slice: x: 4, y: 4, z: 8, core: 2. Of those that a mesh axis runs over, the one named last changes fastest.
Arguments:
- front_entries: float32 [4, 8192, 8192], P('cube', 'row', 'col'), as said below
- child_updates: float32 [4, 2, 4096, 4096], P('cube', None, ('row', 'col')), may hold values from -6 to 6, as said below
- child_index: int32 [4, 2, 64], replicated, may hold values from 0 to 127, as said below
- child_blocks: int32 [4, 2], replicated, may hold values from 32 to 64
Outputs:
- factored: float32 [4, 8192, 8192], P('cube', 'row', 'col')
Inputs may be any that keep to these rules, and one draw needn't show every extreme that they name: `front_entries`: each front is symmetric positive definite in natural numbering. `child_updates`: each contribution block is symmetric. `child_index`: each list names 64 different front blocks; entry t of a list names a front block whose rows lie in a 512-wide block b of front variables with b mod 4 = t div (16).
All inputs are finite; a program needn't handle non-finite values.
Results may differ from a plain program's by a relative error of at most 0.0001.
Values sent between devices are 32-bit elements; how exact they have to be, the bound alone decides.
No kernel may reach another device: no remote copies, remote signals or barrier semaphores. Data moves between devices by JAX's collectives and lax.ppermute only.
A program may use at most 128 MiB of HBM per device.

v0:
```python
import jax
import jax.numpy as jnp
from jax import lax
from jax.sharding import PartitionSpec as P

F = 8192
B = 512
SBLK = 64
CR = 4096
PANELS = 2
HIGHEST_PRECISION = lax.Precision.HIGHEST


def swapped(value, axis, apart):
    mask = 2**apart
    pairs = [(source, source ^ mask) for source in range(lax.axis_size(axis))]
    return lax.ppermute(value, axis, pairs)


def spread_2(block, axis, holder):
    block = jnp.where(lax.axis_index(axis) == holder, block, jnp.zeros_like(block))
    return lax.psum(block, axis)


def storage_position(variable, parts, local_size):
    block = variable // B
    return block % parts * local_size + block // parts * B + variable % B


def natural_variable(local_size, parts, index):
    local = jnp.arange(local_size, dtype=jnp.int32)
    return (local // B * parts + index) * B + local % B


def child_variable(block_lists, offsets):
    return jnp.take(block_lists, offsets // SBLK, axis=1) * SBLK + offsets % SBLK


def solve_panel(rows_in, factor, row_block, panel_step, row_index, root_row, row_slot):
    solved = lax.linalg.triangular_solve(
        factor, rows_in, left_side=False, lower=True, transpose_a=True
    )
    solved = jnp.where((row_block < panel_step)[:, None], 0.0, solved)
    with_pivot = lax.dynamic_update_slice(solved, factor, (row_slot * B, 0))
    return jnp.where(row_index == root_row, with_pivot, solved)


def on_device(front_entries, child_updates, child_index, child_blocks):
    n_row = lax.axis_size("row")
    n_col = lax.axis_size("col")
    row_index = lax.axis_index("row")
    col_index = lax.axis_index("col")
    cube_index = lax.axis_index("cube")
    sibling = jnp.bitwise_xor(cube_index, 1)
    working = front_entries[0]
    rows_here, cols_here = working.shape
    piece_rows = child_updates.shape[2]
    arrived_child = swapped(child_updates[0, 1], "cube", 0)
    pieces = jnp.stack([child_updates[0, 0], arrived_child])
    block_lists = jnp.stack([child_index[cube_index, 0], child_index[sibling, 1]])
    counts = jnp.stack([child_blocks[cube_index, 0], child_blocks[sibling, 1]])
    offsets = jnp.arange(CR, dtype=jnp.int32)
    flat_index = row_index * n_col + col_index
    own_rows = flat_index * piece_rows + jnp.arange(piece_rows, dtype=jnp.int32)
    live_cols = (offsets // SBLK)[None, :] < counts[:, None]
    live_rows = (own_rows // SBLK)[None, :] < counts[:, None]
    values = jnp.where(live_rows[:, :, None] & live_cols[:, None, :], pieces, 0.0)
    col_targets = storage_position(child_variable(block_lists, offsets), n_col, cols_here)

    def widen(child_values, targets):
        return jnp.zeros((piece_rows, F), jnp.float32).at[:, targets].add(child_values)

    spread = jax.vmap(widen)(values, col_targets).reshape(2 * piece_rows, F)
    arrived = lax.all_to_all(spread, "col", split_axis=1, concat_axis=0, tiled=True)
    sources = jnp.arange(n_col, dtype=jnp.int32)
    source_rows = (row_index * n_col + sources)[:, None] * piece_rows + jnp.arange(
        piece_rows, dtype=jnp.int32
    )[None, :]
    natural_rows = child_variable(block_lists, source_rows)
    row_targets = storage_position(jnp.swapaxes(natural_rows, 0, 1), n_row, rows_here).reshape(-1)
    local_rows = row_targets - row_index * rows_here
    working = working.at[local_rows].add(arrived)
    row_block = natural_variable(rows_here, n_row, row_index) // B
    col_block = natural_variable(cols_here, n_col, col_index) // B
    identity = jnp.eye(B, dtype=jnp.float32)
    for panel_step in range(PANELS):
        root_row = panel_step % n_row
        row_slot = panel_step // n_row
        root_col = panel_step % n_col
        col_slot = panel_step // n_col
        diagonal = working[row_slot * B : (row_slot + 1) * B, col_slot * B : (col_slot + 1) * B]
        panel_cols = working
        own_pivot = jnp.where(col_index == root_col, diagonal, identity)
        pivot_block = spread_2(own_pivot, "row", root_row)
        factor = jnp.linalg.cholesky(pivot_block)
        own_lower = solve_panel(
            panel_cols, factor, row_block, panel_step, row_index, root_row, row_slot
        )
        lower_rows = spread_2(own_lower, "col", root_col)
        global_block = 0 + col_index
        block_piece = lax.dynamic_slice_in_dim(lower_rows, global_block // n_row * B, B, 0)
        col_pieces = jnp.where(global_block % n_row == row_index, block_piece, 0.0)
        lower_cols = lax.psum(col_pieces, "row")
        working = working - jnp.dot(
            lower_rows,
            lower_cols.T,
            precision=HIGHEST_PRECISION,
            preferred_element_type=jnp.float32,
        )
        replaced = working.at[:, col_slot * B : (col_slot + 1) * B].set(lower_rows)
        working = jnp.where(col_index == root_col, replaced, working)
    finished = (row_block < PANELS)[:, None] & (col_block >= PANELS)[None, :]
    return jnp.where(finished, 0.0, working)[None]


def solution(mesh):
    in_specs = (P("cube", "row", "col"), P("cube", None, ("row", "col"), None), P(), P())
    out_specs = P("cube", "row", "col")
    return jax.shard_map(
        on_device, mesh=mesh, in_specs=in_specs, out_specs=out_specs, check_vma=False
    )
```

profile of v0, /device:TPU:8, one launch (start us, length us, event | category | flops | bytes accessed | tf_op | source)
XLA Modules:
  0.0 1050.2 jit_solution(9398155492795176346)
XLA Ops:
  6.5 4.8 copy.227
  12.5 2.2 collective-permute-start
  16.2 14.1 %gather_fusion.1 = s32[4096,2]{1,0:T(8,128)} fusion(s32[2,64]{0,1:T(8,128)S(1)} %copy.127, s32[4096]{0:T(1024)S(1)} %broadcast_clamp_fusion), kind=kCustom, calls=%fused_computation.1 | custom fusion | bytes 81920 | tf_op jit(solution)/shard_map/jit(_take)/gather | solution.py:36
  30.3 7.2 compare_select_fusion
  39.2 1.5 copy.179
  42.0 2.6 broadcast_select_fusion.2
  44.6 2.2 copy.133
  47.0 1.6 fusion.23
  48.5 2.7 copy.174
  51.3 48.2 %scatter_custom_fusion.1 = f32[16384,64]{1,0:T(8,128)} fusion(s32[8192]{0:T(1024)S(1)} %bitcast.172, f32[8192,64]{1,0:T(8,128)} %bitcast.167, f32[]{:T(128)} %constant.447.clone.1), kind=kCustom, calls=%fused_computation.11 | custom fusion | flops 524288 | bytes 4194816
  99.5 8.7 copy.175
  108.1 4.6 copy.137
  112.8 3.3 copy.182
  116.0 4.4 copy.138
  120.4 6.9 all-to-all-start
  127.6 2.8 gather_fusion
  131.0 90.6 %all-to-all-done = f32[128,16,512]{2,0,1:T(8,128)} async-done(((f32[128,16,512]{2,0,1:T(8,128)}), f32[128,16,512]{2,0,1:T(8,128)}, u32[]{:S(2)}, u32[]{:S(2)}) %all-to-all-start) | async-done | bytes 4194336 | tf_op jit(solution)/shard_map/all_to_all | solution.py:74
  221.6 17.4 %scatter_fusion = f32[2048,512]{1,0:T(8,128)} fusion(f32[2048,512]{1,0:T(8,128)} %bitcast.156, s32[2048]{0:T(1024)S(1)} %bitcast.171, f32[2048,512]{1,0:T(8,128)} %bitcast.19), kind=kCustom, calls=%fused_computation.2 | custom fusion | flops 1048576 | bytes 12591104 | tf_op jit(solution)/shard_map/scatter-add | solution.py:82
  239.0 5.4 copy.139
  244.4 2.4 fusion.38
  247.3 50.5 %all-reduce.8.cloned.1.call-done = f32[512,512]{0,1:T(8,128)} async-done(((f32[512,512]{0,1:T(8,128)}), f32[512,512]{0,1:T(8,128)}) %all-reduce.8.cloned.1.call-update) | async-done | bytes 1048592 | tf_op jit(solution)/shard_map/psum | solution.py:22
  297.8 1.6 copy.140
  299.3 1.4 fusion.47
  300.8 11.7 %cholesky.286 = f32[128,128]{1,0:T(8,128)S(1)} custom-call(f32[128,128]{1,0:T(8,128)S(1)} %cholesky.426), custom_call_target="Cholesky" | custom-call | tf_op jit(solution)/shard_map/jit(cholesky)/cholesky | solution.py:95
  312.5 9.8 custom-call.27
  323.0 11.7 %cholesky.305 = f32[128,128]{1,0:T(8,128)S(1)} custom-call(f32[128,128]{1,0:T(8,128)S(1)} %cholesky.430), custom_call_target="Cholesky" | custom-call | tf_op jit(solution)/shard_map/jit(cholesky)/cholesky | solution.py:95
  335.1 9.9 custom-call.28
  346.2 11.7 %cholesky.326 = f32[128,128]{1,0:T(8,128)S(1)} custom-call(f32[128,128]{1,0:T(8,128)S(1)} %cholesky.435), custom_call_target="Cholesky" | custom-call | tf_op jit(solution)/shard_map/jit(cholesky)/cholesky | solution.py:95
  358.0 9.8 custom-call.29
  368.6 11.9 %cholesky.343 = f32[128,128]{1,0:T(8,128)S(1)} custom-call(f32[128,128]{1,0:T(8,128)S(1)} %convolution_subtract_fusion.9), custom_call_target="Cholesky" | custom-call | tf_op jit(solution)/shard_map/jit(cholesky)/cholesky | solution.py:95
  385.4 8.3 while.8
  393.6 39.3 %custom-call.30 = f32[4,128,128]{1,2,0:T(8,128)S(1)} custom-call(f32[4,128,128]{2,1,0:T(8,128)S(1)} %get-tuple-element.61), custom_call_target="InvertDiagBlocksLowerTriangular" | custom-call | tf_op jit(solution)/shard_map/triangular_solve/custom-call.3 | solution.py:40
  433.0 2.4 fusion.44
  435.4 3.0 convolution_subtract_fusion.3
  439.6 3.5 convolution_subtract_fusion.1
  444.1 5.6 fusion.17
  451.7 2.6 broadcast_select_fusion.1
  454.3 122.6 %all-reduce.10.cloned.1.call-done = f32[2048,512]{0,1:T(8,128)} async-done(((f32[2048,512]{0,1:T(8,128)}), f32[2048,512]{0,1:T(8,128)}) %all-reduce.10.cloned.1.call-update) | async-done | bytes 4194320 | tf_op jit(solution)/shard_map/psum | solution.py:22
  576.9 2.3 dynamic-slice_select_fusion.1
  579.3 50.9 %all-reduce.12.cloned.1.call-done = f32[512,512]{0,1:T(8,128)} async-done(((f32[512,512]{0,1:T(8,128)}), f32[512,512]{0,1:T(8,128)}) %all-reduce.12.cloned.1.call-update) | async-done | bytes 1048592 | tf_op jit(solution)/shard_map/psum | solution.py:103
  630.2 11.9 %subtract_select_fusion = f32[2048,512]{0,1:T(8,128)S(1)} fusion(f32[2048,512]{0,1:T(8,128)} %all-reduce.10.cloned.1.call-done, f32[2048,512]{0,1:T(8,128)} %copy.139, f32[512,512]{0,1:T(8,128)} %all-reduce.12.cloned.1.call-done, pred[]{:T(512)S(6)} %eq.46), kind=kOutput, calls=%fused_computation.14 | convolution fusion | flops 6444548096 | bytes 13631489 | tf_op jit(solution)/shard_map/dot_general | solution.py:104
  642.1 2.0 copy-done.1
  645.6 51.7 %all-reduce.14.cloned.1.call-done = f32[512,512]{0,1:T(8,128)} async-done(((f32[512,512]{0,1:T(8,128)}), f32[512,512]{0,1:T(8,128)}) %all-reduce.14.cloned.1.call-update) | async-done | bytes 1048592 | tf_op jit(solution)/shard_map/psum | solution.py:22
  697.3 1.6 copy.151
  698.8 1.4 fusion.46
  700.3 11.7 %cholesky.358 = f32[128,128]{1,0:T(8,128)S(1)} custom-call(f32[128,128]{1,0:T(8,128)S(1)} %cholesky.439), custom_call_target="Cholesky" | custom-call | tf_op jit(solution)/shard_map/jit(cholesky)/cholesky | solution.py:95
  712.0 9.8 custom-call.31
  722.5 11.7 %cholesky.377 = f32[128,128]{1,0:T(8,128)S(1)} custom-call(f32[128,128]{1,0:T(8,128)S(1)} %cholesky.443), custom_call_target="Cholesky" | custom-call | tf_op jit(solution)/shard_map/jit(cholesky)/cholesky | solution.py:95
  734.6 10.2 custom-call.32
  745.9 11.7 %cholesky.398 = f32[128,128]{1,0:T(8,128)S(1)} custom-call(f32[128,128]{1,0:T(8,128)S(1)} %cholesky.448), custom_call_target="Cholesky" | custom-call | tf_op jit(solution)/shard_map/jit(cholesky)/cholesky | solution.py:95
  757.8 9.8 custom-call.33
  768.4 11.9 %cholesky.415 = f32[128,128]{1,0:T(8,128)S(1)} custom-call(f32[128,128]{1,0:T(8,128)S(1)} %convolution_subtract_fusion.8), custom_call_target="Cholesky" | custom-call | tf_op jit(solution)/shard_map/jit(cholesky)/cholesky | solution.py:95
  785.8 8.6 while.9
  794.4 39.3 %custom-call.34 = f32[4,128,128]{1,2,0:T(8,128)S(1)} custom-call(f32[4,128,128]{2,1,0:T(8,128)S(1)} %get-tuple-element.62), custom_call_target="InvertDiagBlocksLowerTriangular" | custom-call | tf_op jit(solution)/shard_map/triangular_solve/custom-call.3 | solution.py:40
  833.7 2.4 fusion.41
  836.1 2.3 convolution_subtract_fusion.2
  839.5 1.3 convolution_subtract_fusion
  842.0 2.2 fusion.14
  846.2 2.5 broadcast_select_fusion
  848.8 122.5 %all-reduce.16.cloned.1.call-done = f32[2048,512]{0,1:T(8,128)} async-done(((f32[2048,512]{0,1:T(8,128)}), f32[2048,512]{0,1:T(8,128)}) %all-reduce.16.cloned.1.call-update) | async-done | bytes 4194320 | tf_op jit(solution)/shard_map/psum | solution.py:22
  971.3 2.3 dynamic-slice_select_fusion
  973.6 50.9 %all-reduce.18.cloned.1.call-done = f32[512,512]{0,1:T(8,128)} async-done(((f32[512,512]{0,1:T(8,128)}), f32[512,512]{0,1:T(8,128)}) %all-reduce.18.cloned.1.call-update) | async-done | bytes 1048592 | tf_op jit(solution)/shard_map/psum | solution.py:103
  1024.5 13.3 %select_bitcast_fusion = f32[1,2048,512]{1,2,0:T(8,128)} fusion(f32[2048,512]{0,1:T(8,128)} %all-reduce.16.cloned.1.call-done, f32[2048,512]{0,1:T(8,128)} %copy-done.1, f32[512,512]{0,1:T(8,128)} %all-reduce.18.cloned.1.call-done, pred[]{:T(512)S(6)} %eq.44, pred[2048]{0:T(1024)(128)(4,1)S(1)} %broadcast_compare_fusion.1, pred[512]{0:T(512)(128)(4,1)S(1)} %fusion.135), kind=kOutput, calls=%fused_computation.13 | convolution fusion | flops 6446645248 | bytes 13634049 | tf_op jit(solution)/shard_map/dot_general | solution.py:104
  1037.8 5.3 copy.164
  (170 shorter events, 44.9 us)
Async XLA Ops:
  6.5 4.8 copy-start.3
  11.3 3.4 copy-start.4
  12.5 25.7 %copy-start.6 = (s32[2]{0:T(128)S(1)}, s32[2]{0:T(128)}, u32[]{:S(2)}) copy-start(s32[2]{0:T(128)} %constant.461) | copy-start | bytes 28
  12.5 34.5 %collective-permute-start = (f32[64,4096]{1,0:T(8,128)}, f32[64,4096]{1,0:T(8,128)}, u32[]{:S(2)}, u32[]{:S(2)}) collective-permute-start(f32[64,4096]{1,0:T(8,128)} %get-tuple-element.124), channel_id=1, source_target_pairs={{0,64},{64,0},{128,192},{192,128},{1,65},{65,1},{129,193},{193,129... | collective-permute-start | bytes 3145736 | tf_op jit(solution)/shard_map/ppermute | solution.py:17
  30.3 8.7 copy-start.5
  120.4 101.2 %all-to-all-start = ((f32[128,16,512]{2,0,1:T(8,128)}), f32[128,16,512]{2,0,1:T(8,128)}, u32[]{:S(2)}, u32[]{:S(2)}) async-start(f32[128,16,512]{2,0,1:T(8,128)} %copy.138), calls=%async_computation | async-start | bytes 8388608 | tf_op jit(solution)/shard_map/all_to_all | solution.py:74
  127.3 170.4 %all-reduce.8.cloned.1.call-start = ((), (), s32[]{:S(2)}) async-start(), calls=%async_computation.1 | async-start | bytes 2097152 | tf_op jit(solution)/shard_map/psum | solution.py:22
  246.8 330.1 %all-reduce.10.cloned.1.call-start = ((), (), s32[]{:S(2)}) async-start(), calls=%async_computation.2 | async-start | bytes 8388608 | tf_op jit(solution)/shard_map/psum | solution.py:22
  433.0 6.6 copy-start
  454.3 175.9 %all-reduce.12.cloned.1.call-start = ((), (), s32[]{:S(2)}) async-start(), calls=%async_computation.3 | async-start | bytes 2097152 | tf_op jit(solution)/shard_map/psum | solution.py:103
  579.2 118.0 %all-reduce.14.cloned.1.call-start = ((), (), s32[]{:S(2)}) async-start(), calls=%async_computation.4 | async-start | bytes 2097152 | tf_op jit(solution)/shard_map/psum | solution.py:22
  642.1 2.0 copy-start.1
  645.3 325.9 %all-reduce.16.cloned.1.call-start = ((), (), s32[]{:S(2)}) async-start(), calls=%async_computation.5 | async-start | bytes 8388608 | tf_op jit(solution)/shard_map/psum | solution.py:22
  833.7 5.8 copy-start.2
  848.7 175.8 %all-reduce.18.cloned.1.call-start = ((), (), s32[]{:S(2)}) async-start(), calls=%async_computation.6 | async-start | bytes 2097152 | tf_op jit(solution)/shard_map/psum | solution.py:103
Sparse Core Ops, SparseCore 0:
  246.9 50.8 all-reduce.7
  454.4 122.4 all-reduce.9
  579.4 50.7 all-reduce.11
  645.4 51.7 all-reduce.13
  848.8 122.3 all-reduce.15
  973.7 50.7 all-reduce.17
where the time goes:
time: 1060 us; the launch traced here: 1050 us
  waiting for transfers between devices  540 us (51%)
  other arithmetic  334 us (32%)
  local copies, waits for them, and re-layouts  87.2 us (8%)
  matrix products  59.1 us (6%)
  between operations  19.6 us (2%)
    psum x4, waiting for transfers between devices, spread_2(): return lax.psum(block, axis)  347 us
    another operation x29, other arithmetic, on_device(): factor = jnp.linalg.cholesky(pivot_block)  158 us
    psum x2, waiting for transfers between devices, on_device(): lower_cols = lax.psum(col_pieces, 'row')  102 us
    all_to_all x1, waiting for transfers between devices, on_device(): lax.all_to_all(spread, 'col', split_axis=1, concat_axis=0, tiled=True)  90.6 us
    another operation x5, other arithmetic, solve_panel(): lax.linalg.triangular_solve(factor, rows_in, left_side=False, lower=True,...  78.9 us
    unnamed x4, other arithmetic  51.1 us
    another operation x14, matrix products, solve_panel(): lax.linalg.triangular_solve(factor, rows_in, left_side=False, lower=True,...  29.3 us
    dot_general x2, matrix products, on_device(): jnp.dot(lower_rows, lower_cols.T, precision=HIGHEST_PRECISION, preferred_...  25.2 us
  transfers between devices with their start and end apart: 8, of which 7 were waited for; matrix products, arithmetic and copies ran while one was open for 3% of the time, Pallas kernels for 0%

commit v1 on v0

--- a/solution.py
+++ b/solution.py
@@ -100,7 +100,11 @@
         global_block = 0 + col_index
         block_piece = lax.dynamic_slice_in_dim(lower_rows, global_block // n_row * B, B, 0)
         col_pieces = jnp.where(global_block % n_row == row_index, block_piece, 0.0)
-        lower_cols = lax.psum(col_pieces, "row")
+        lower_cols = col_pieces
+        for hop in (1, 2):
+            lower_cols = lower_cols + lax.ppermute(
+                lower_cols, "row", [(dev, dev ^ hop) for dev in range(4)]
+            )
         working = working - jnp.dot(
             lower_rows,
             lower_cols.T,

time: 1060 us -> 1050 us (level)
  waiting for transfers between devices: 540 us -> 527 us
    psum x2 -> x0, waiting for transfers between devices: 102 us -> none  [on_device(): lower_cols = lax.psum(col_pieces, 'row')]
    ppermute x0 -> x4, waiting for transfers between devices: none -> 89 us  [on_device(): lax.ppermute(lower_cols, 'row', [(dev, dev ^ hop) for dev in range(4)])]
    unnamed x22 -> x24, local copies, waits for them, and re-layouts: 23.1 us -> 23.1 us
  transfers between devices with their start and end apart: 8 -> 10, of which waited for: 7 -> 9; matrix products, arithmetic and copies ran while one was open for 3% -> 3% of each run, Pallas kernels for 0% -> 0%
where the time goes in v1:
time: 1050 us; the launch traced here: 1040 us
  waiting for transfers between devices  527 us (50%)
  other arithmetic  335 us (32%)
  local copies, waits for them, and re-layouts  87.2 us (8%)
  matrix products  54.8 us (5%)
  between operations  19.2 us (2%)
  starting transfers between devices  19.1 us (2%)
    psum x4, waiting for transfers between devices, spread_2(): return lax.psum(block, axis)  347 us
    another operation x29, other arithmetic, on_device(): factor = jnp.linalg.cholesky(pivot_block)  158 us
    all_to_all x1, waiting for transfers between devices, on_device(): lax.all_to_all(spread, 'col', split_axis=1, concat_axis=0, tiled=True)  90.6 us
    ppermute x4, waiting for transfers between devices, on_device(): lax.ppermute(lower_cols, 'row', [(dev, dev ^ hop) for dev in range(4)])  89 us
    another operation x5, other arithmetic, solve_panel(): lax.linalg.triangular_solve(factor, rows_in, left_side=False, lower=True,...  78.9 us
    unnamed x4, other arithmetic  51.1 us
    another operation x14, matrix products, solve_panel(): lax.linalg.triangular_solve(factor, rows_in, left_side=False, lower=True,...  28.2 us
    unnamed x24, local copies, waits for them, and re-layouts  23.1 us
  transfers between devices with their start and end apart: 10, of which 9 were waited for; matrix products, arithmetic and copies ran while one was open for 3% of the time, Pallas kernels for 0%

profile of v1, /device:TPU:8, one launch (start us, length us, event | category | flops | bytes accessed | tf_op | source)
XLA Modules:
  0.0 1043.1 jit_solution(8816265804122150275)
XLA Ops:
  6.5 4.8 copy.225
  12.5 2.2 collective-permute-start
  16.2 14.1 %gather_fusion.1 = s32[4096,2]{1,0:T(8,128)} fusion(s32[2,64]{0,1:T(8,128)S(1)} %copy.127, s32[4096]{0:T(1024)S(1)} %broadcast_clamp_fusion), kind=kCustom, calls=%fused_computation.1 | custom fusion | bytes 81920 | tf_op jit(solution)/shard_map/jit(_take)/gather | solution.py:36
  30.3 7.2 compare_select_fusion
  39.2 1.5 copy.179
  42.0 2.6 broadcast_select_fusion.2
  44.6 2.2 copy.133
  47.0 1.6 fusion.20
  48.5 2.7 copy.174
  51.3 48.2 %scatter_custom_fusion.1 = f32[16384,64]{1,0:T(8,128)} fusion(s32[8192]{0:T(1024)S(1)} %bitcast.167, f32[8192,64]{1,0:T(8,128)} %bitcast.162, f32[]{:T(128)} %constant.447.clone.1), kind=kCustom, calls=%fused_computation.11 | custom fusion | flops 524288 | bytes 4194816
  99.5 8.7 copy.175
  108.1 4.6 copy.137
  112.8 3.3 copy.182
  116.0 4.4 copy.138
  120.4 6.9 all-to-all-start
  127.6 2.8 gather_fusion
  131.0 90.6 %all-to-all-done = f32[128,16,512]{2,0,1:T(8,128)} async-done(((f32[128,16,512]{2,0,1:T(8,128)}), f32[128,16,512]{2,0,1:T(8,128)}, u32[]{:S(2)}, u32[]{:S(2)}) %all-to-all-start) | async-done | bytes 4194336 | tf_op jit(solution)/shard_map/all_to_all | solution.py:74
  221.6 17.4 %scatter_fusion = f32[2048,512]{1,0:T(8,128)} fusion(f32[2048,512]{1,0:T(8,128)} %bitcast.151, s32[2048]{0:T(1024)S(1)} %bitcast.166, f32[2048,512]{1,0:T(8,128)} %bitcast.19), kind=kCustom, calls=%fused_computation.2 | custom fusion | flops 1048576 | bytes 12591104 | tf_op jit(solution)/shard_map/scatter-add | solution.py:82
  239.0 5.4 copy.139
  244.4 2.4 fusion.36
  247.3 50.5 %all-reduce.6.cloned.1.call-done = f32[512,512]{0,1:T(8,128)} async-done(((f32[512,512]{0,1:T(8,128)}), f32[512,512]{0,1:T(8,128)}) %all-reduce.6.cloned.1.call-update) | async-done | bytes 1048592 | tf_op jit(solution)/shard_map/psum | solution.py:22
  297.8 1.6 copy.140
  300.8 11.7 %cholesky.286 = f32[128,128]{1,0:T(8,128)S(1)} custom-call(f32[128,128]{1,0:T(8,128)S(1)} %cholesky.426), custom_call_target="Cholesky" | custom-call | tf_op jit(solution)/shard_map/jit(cholesky)/cholesky | solution.py:95
  312.5 9.8 custom-call.27
  323.0 11.7 %cholesky.305 = f32[128,128]{1,0:T(8,128)S(1)} custom-call(f32[128,128]{1,0:T(8,128)S(1)} %cholesky.430), custom_call_target="Cholesky" | custom-call | tf_op jit(solution)/shard_map/jit(cholesky)/cholesky | solution.py:95
  335.1 9.9 custom-call.28
  346.2 11.7 %cholesky.326 = f32[128,128]{1,0:T(8,128)S(1)} custom-call(f32[128,128]{1,0:T(8,128)S(1)} %cholesky.435), custom_call_target="Cholesky" | custom-call | tf_op jit(solution)/shard_map/jit(cholesky)/cholesky | solution.py:95
  358.0 9.8 custom-call.29
  368.6 11.9 %cholesky.343 = f32[128,128]{1,0:T(8,128)S(1)} custom-call(f32[128,128]{1,0:T(8,128)S(1)} %convolution_subtract_fusion.7), custom_call_target="Cholesky" | custom-call | tf_op jit(solution)/shard_map/jit(cholesky)/cholesky | solution.py:95
  385.4 8.3 while.8
  393.6 39.3 %custom-call.30 = f32[4,128,128]{1,2,0:T(8,128)S(1)} custom-call(f32[4,128,128]{2,1,0:T(8,128)S(1)} %get-tuple-element.61), custom_call_target="InvertDiagBlocksLowerTriangular" | custom-call | tf_op jit(solution)/shard_map/triangular_solve/custom-call.3 | solution.py:40
  433.0 2.4 fusion.45
  435.4 3.0 convolution_subtract_fusion.1
  439.6 3.5 convolution_subtract_fusion
  444.1 5.6 fusion.14
  451.7 2.6 broadcast_select_fusion.1
  454.3 122.6 %all-reduce.8.cloned.1.call-done = f32[2048,512]{0,1:T(8,128)} async-done(((f32[2048,512]{0,1:T(8,128)}), f32[2048,512]{0,1:T(8,128)}) %all-reduce.8.cloned.1.call-update) | async-done | bytes 4194320 | tf_op jit(solution)/shard_map/psum | solution.py:22
  578.2 1.6 collective-permute-start.1
  579.8 22.7 %collective-permute-done.1 = f32[512,512]{0,1:T(8,128)S(1)} collective-permute-done((f32[512,512]{0,1:T(8,128)S(1)}, f32[512,512]{0,1:T(8,128)S(1)}, u32[]{:S(2)}, u32[]{:S(2)}) %collective-permute-start.1) | collective-permute-done | bytes 1048608 | tf_op jit(solution)/shard_map/ppermute | solution.py:105
  604.0 3.1 collective-permute-start.2
  607.0 21.8 %collective-permute-done.2 = f32[512,512]{0,1:T(8,128)S(1)} collective-permute-done((f32[512,512]{0,1:T(8,128)S(1)}, f32[512,512]{0,1:T(8,128)S(1)}, u32[]{:S(2)}, u32[]{:S(2)}) %collective-permute-start.2) | collective-permute-done | bytes 1048608 | tf_op jit(solution)/shard_map/ppermute | solution.py:105
  628.8 10.5 %subtract_select_fusion = f32[2048,512]{0,1:T(8,128)S(1)} fusion(f32[2048,512]{0,1:T(8,128)} %all-reduce.8.cloned.1.call-done, f32[2048,512]{0,1:T(8,128)} %copy.139, pred[]{:T(512)S(6)} %eq.46, f32[512,512]{0,1:T(8,128)S(1)} %fusion.159, f32[512,512]{0,1:T(8,128)S(1)} %collective-permute-done.2), kind=kOutput, calls=%fused_computation.14 | convolution fusion | flops 6444810240 | bytes 14680065 | tf_op jit(solution)/shard_map/dot_general | solution.py:108
  639.3 2.0 copy-done.1
  642.8 51.7 %all-reduce.10.cloned.1.call-done = f32[512,512]{0,1:T(8,128)} async-done(((f32[512,512]{0,1:T(8,128)}), f32[512,512]{0,1:T(8,128)}) %all-reduce.10.cloned.1.call-update) | async-done | bytes 1048592 | tf_op jit(solution)/shard_map/psum | solution.py:22
  694.5 1.6 copy.151
  697.5 11.7 %cholesky.358 = f32[128,128]{1,0:T(8,128)S(1)} custom-call(f32[128,128]{1,0:T(8,128)S(1)} %cholesky.439), custom_call_target="Cholesky" | custom-call | tf_op jit(solution)/shard_map/jit(cholesky)/cholesky | solution.py:95
  709.3 9.8 custom-call.31
  719.8 11.7 %cholesky.377 = f32[128,128]{1,0:T(8,128)S(1)} custom-call(f32[128,128]{1,0:T(8,128)S(1)} %cholesky.443), custom_call_target="Cholesky" | custom-call | tf_op jit(solution)/shard_map/jit(cholesky)/cholesky | solution.py:95
  731.9 10.2 custom-call.32
  743.1 11.7 %cholesky.398 = f32[128,128]{1,0:T(8,128)S(1)} custom-call(f32[128,128]{1,0:T(8,128)S(1)} %cholesky.448), custom_call_target="Cholesky" | custom-call | tf_op jit(solution)/shard_map/jit(cholesky)/cholesky | solution.py:95
  755.0 9.8 custom-call.33
  765.6 11.9 %cholesky.415 = f32[128,128]{1,0:T(8,128)S(1)} custom-call(f32[128,128]{1,0:T(8,128)S(1)} %convolution_subtract_fusion.6), custom_call_target="Cholesky" | custom-call | tf_op jit(solution)/shard_map/jit(cholesky)/cholesky | solution.py:95
  783.0 8.6 while.9
  791.6 39.3 %custom-call.34 = f32[4,128,128]{1,2,0:T(8,128)S(1)} custom-call(f32[4,128,128]{2,1,0:T(8,128)S(1)} %get-tuple-element.62), custom_call_target="InvertDiagBlocksLowerTriangular" | custom-call | tf_op jit(solution)/shard_map/triangular_solve/custom-call.3 | solution.py:40
  831.0 2.4 fusion.42
  838.1 2.2 fusion.8
  842.3 2.5 broadcast_select_fusion
  844.9 122.5 %all-reduce.12.cloned.1.call-done = f32[2048,512]{0,1:T(8,128)} async-done(((f32[2048,512]{0,1:T(8,128)}), f32[2048,512]{0,1:T(8,128)}) %all-reduce.12.cloned.1.call-update) | async-done | bytes 4194320 | tf_op jit(solution)/shard_map/psum | solution.py:22
  968.9 1.6 collective-permute-start.3
  970.4 22.7 %collective-permute-done.3 = f32[512,512]{0,1:T(8,128)S(1)} collective-permute-done((f32[512,512]{0,1:T(8,128)S(1)}, f32[512,512]{0,1:T(8,128)S(1)}, u32[]{:S(2)}, u32[]{:S(2)}) %collective-permute-start.3) | collective-permute-done | bytes 1048608 | tf_op jit(solution)/shard_map/ppermute | solution.py:105
  994.6 3.1 collective-permute-start.4
  997.7 21.8 %collective-permute-done.4 = f32[512,512]{0,1:T(8,128)S(1)} collective-permute-done((f32[512,512]{0,1:T(8,128)S(1)}, f32[512,512]{0,1:T(8,128)S(1)}, u32[]{:S(2)}, u32[]{:S(2)}) %collective-permute-start.4) | collective-permute-done | bytes 1048608 | tf_op jit(solution)/shard_map/ppermute | solution.py:105
  1019.5 11.5 %select_bitcast_fusion = f32[1,2048,512]{1,2,0:T(8,128)} fusion(f32[2048,512]{0,1:T(8,128)} %all-reduce.12.cloned.1.call-done, f32[2048,512]{0,1:T(8,128)S(1)} %copy-done.3, pred[]{:T(512)S(6)} %eq.44, pred[2048]{0:T(1024)(128)(4,1)S(1)} %broadcast_compare_fusion.1, pred[512]{0:T(512)(128)(4,1)S(1)} %fusion.136, f32[512,512]{0,1:T(8,128)S(1)} %fusion.158, ...), kind=kOutput, calls=%fused_computation.13 | convolution fusion | flops 6446907392 | bytes 14682625 | tf_op jit(solution)/shard_map/dot_general | solution.py:108
  1031.0 5.3 copy.164
  (176 shorter events, 55.9 us)
Async XLA Ops:
  6.5 4.8 copy-start.4
  11.3 3.4 copy-start.5
  12.5 25.7 %copy-start.7 = (s32[2]{0:T(128)S(1)}, s32[2]{0:T(128)}, u32[]{:S(2)}) copy-start(s32[2]{0:T(128)} %constant.461) | copy-start | bytes 28
  12.5 34.5 %collective-permute-start = (f32[64,4096]{1,0:T(8,128)}, f32[64,4096]{1,0:T(8,128)}, u32[]{:S(2)}, u32[]{:S(2)}) collective-permute-start(f32[64,4096]{1,0:T(8,128)} %get-tuple-element.124), channel_id=1, source_target_pairs={{0,64},{64,0},{128,192},{192,128},{1,65},{65,1},{129,193},{193,129... | collective-permute-start | bytes 3145736 | tf_op jit(solution)/shard_map/ppermute | solution.py:17
  30.3 8.7 copy-start.6
  120.4 101.2 %all-to-all-start = ((f32[128,16,512]{2,0,1:T(8,128)}), f32[128,16,512]{2,0,1:T(8,128)}, u32[]{:S(2)}, u32[]{:S(2)}) async-start(f32[128,16,512]{2,0,1:T(8,128)} %copy.138), calls=%async_computation | async-start | bytes 8388608 | tf_op jit(solution)/shard_map/all_to_all | solution.py:74
  127.3 170.4 %all-reduce.6.cloned.1.call-start = ((), (), s32[]{:S(2)}) async-start(), calls=%async_computation.1 | async-start | bytes 2097152 | tf_op jit(solution)/shard_map/psum | solution.py:22
  246.8 330.1 %all-reduce.8.cloned.1.call-start = ((), (), s32[]{:S(2)}) async-start(), calls=%async_computation.2 | async-start | bytes 8388608 | tf_op jit(solution)/shard_map/psum | solution.py:22
  433.0 6.6 copy-start
  454.3 240.3 %all-reduce.10.cloned.1.call-start = ((), (), s32[]{:S(2)}) async-start(), calls=%async_computation.3 | async-start | bytes 2097152 | tf_op jit(solution)/shard_map/psum | solution.py:22
  578.2 24.3 %collective-permute-start.1 = (f32[512,512]{0,1:T(8,128)S(1)}, f32[512,512]{0,1:T(8,128)S(1)}, u32[]{:S(2)}, u32[]{:S(2)}) collective-permute-start(f32[512,512]{0,1:T(8,128)S(1)} %dynamic-slice_select_fusion.1), channel_id=1, source_target_pairs={{0,16},{16,0},{32,48},{48,32},{1,17},{17,1},{33,49},{49,33},{2,18}... | collective-permute-start | bytes 3145736 | tf_op jit(solution)/shard_map/ppermute | solution.py:105
  604.0 24.9 %collective-permute-start.2 = (f32[512,512]{0,1:T(8,128)S(1)}, f32[512,512]{0,1:T(8,128)S(1)}, u32[]{:S(2)}, u32[]{:S(2)}) collective-permute-start(f32[512,512]{0,1:T(8,128)S(1)} %fusion.159), channel_id=1, source_target_pairs={{0,32},{16,48},{32,0},{48,16},{1,33},{17,49},{33,1},{49,17},{2,34}... | collective-permute-start | bytes 3145736 | tf_op jit(solution)/shard_map/ppermute | solution.py:105
  639.3 2.0 copy-start.1
  642.5 324.9 %all-reduce.12.cloned.1.call-start = ((), (), s32[]{:S(2)}) async-start(), calls=%async_computation.4 | async-start | bytes 8388608 | tf_op jit(solution)/shard_map/psum | solution.py:22
  830.9 3.5 copy-start.2
  967.4 52.1 %copy-start.3 = (f32[2048,512]{0,1:T(8,128)S(1)}, f32[2048,512]{0,1:T(8,128)}, u32[]{:S(2)}) copy-start(f32[2048,512]{0,1:T(8,128)} %copy-done.1) | copy-start | bytes 12582916
  968.9 24.3 %collective-permute-start.3 = (f32[512,512]{0,1:T(8,128)S(1)}, f32[512,512]{0,1:T(8,128)S(1)}, u32[]{:S(2)}, u32[]{:S(2)}) collective-permute-start(f32[512,512]{0,1:T(8,128)S(1)} %dynamic-slice_select_fusion), channel_id=1, source_target_pairs={{0,16},{16,0},{32,48},{48,32},{1,17},{17,1},{33,49},{49,33},{2,18}... | collective-permute-start | bytes 3145736 | tf_op jit(solution)/shard_map/ppermute | solution.py:105
  994.6 24.9 %collective-permute-start.4 = (f32[512,512]{0,1:T(8,128)S(1)}, f32[512,512]{0,1:T(8,128)S(1)}, u32[]{:S(2)}, u32[]{:S(2)}) collective-permute-start(f32[512,512]{0,1:T(8,128)S(1)} %fusion.158), channel_id=1, source_target_pairs={{0,32},{16,48},{32,0},{48,16},{1,33},{17,49},{33,1},{49,17},{2,34}... | collective-permute-start | bytes 3145736 | tf_op jit(solution)/shard_map/ppermute | solution.py:105
Sparse Core Ops, SparseCore 0:
  246.9 50.8 all-reduce.5
  454.4 122.4 all-reduce.7
  642.6 51.8 all-reduce.9
  845.0 122.3 all-reduce.11
